TPU v7x, 32 devices: a whole 2x2x4 slice. The times are simulated.
32 devices in a mesh: dp: 8 (over y, x, core), mp: 4 (over z).
Axes of the slice: x: 2, y: 2, z: 4, core: 2. Of those that a mesh axis runs over, the one named last changes fastest.
Arguments:
- tokens: bfloat16 [320, 4096], P('dp'), may hold values from -6 to 6
- attn_gain: float32 [4096], replicated, may hold values from 0.1 to 1.9
- head_gain: float32 [4096], replicated, may hold values from 0.1 to 1.9
- qkv_weight: bfloat16 [4096, 3, 4096], P('dp', None, 'mp'), may hold values from -0.09375 to 0.09375
- out_weight: bfloat16 [4096, 4096], P('mp', 'dp'), may hold values from -0.09375 to 0.09375
- head_weight: bfloat16 [4096, 1024], P('mp'), may hold values from -0.09375 to 0.09375
- key_cache: bfloat16 [320, 64, 4096], P('dp', None, 'mp'), may hold values from -400 to 400
- value_cache: bfloat16 [320, 64, 4096], P('dp', None, 'mp'), may hold values from -6 to 6
- parents: int32 [320], P('dp'), may hold values from 0 to 19
- allowed: int32 [320, 2], P('dp'), may hold values from 0 to 7, all different within a row
Outputs:
- new_stream: bfloat16 [320, 4096], P('dp')
- next_logits: float32 [320, 256], P('dp', 'mp')
Inputs may be any that keep to these rules, and one draw needn't show every extreme that they name: `parents`: a beam's parent is a beam of the same query. `allowed`: the 2 block ids of a beam differ.
All inputs are finite; a program needn't handle non-finite values.
Results may differ from a plain program's by a relative error of at most 0.017.
Values may be sent and summed in bfloat16 or wider, within the bound.
No kernel may reach another device: no remote copies, remote signals or barrier semaphores. Data moves between devices by JAX's collectives and lax.ppermute only.
A program may use at most 128 MiB of HBM per device.

v0:
```python
import jax
import jax.numpy as jnp
from jax import lax
from jax.sharding import PartitionSpec as P

HEAD = 128
BEAMS = 20
BLOCK = 128


def root_norm(values, gain_vec):
    float_values = values.astype(jnp.float32)
    factor = lax.rsqrt(jnp.mean(float_values * float_values, axis=-1, keepdims=True) + 1e-06)
    return float_values * factor * gain_vec


def select_blocks(whole_logits, allowed):
    block_count = whole_logits.shape[1] // BLOCK
    block_list = whole_logits.reshape(whole_logits.shape[0], block_count, BLOCK)
    one_hot_rows = (
        allowed[:, :, None] == jnp.arange(block_count, dtype=jnp.int32)[None, None, :]
    ).astype(jnp.float32)
    selected_token = jnp.einsum(
        "ioh,ihp->iop", one_hot_rows, block_list, precision=lax.Precision.HIGHEST
    )
    return selected_token.reshape(whole_logits.shape[0], -1)


def on_device(
    tokens,
    attn_gain,
    head_gain,
    qkv_weight,
    out_weight,
    head_weight,
    key_cache,
    value_cache,
    parents,
    allowed,
):
    row_count = tokens.shape[0]
    normed = root_norm(tokens, attn_gain).astype(jnp.bfloat16)
    spread = lax.all_to_all(normed, "dp", split_axis=1, concat_axis=0, tiled=True)
    depth_part = qkv_weight.shape[0]
    head_width = qkv_weight.shape[2]
    flat_qkv = qkv_weight.reshape(depth_part, 3 * head_width)
    projected = lax.psum_scatter(
        jnp.dot(spread, flat_qkv, preferred_element_type=jnp.float32),
        "dp",
        scatter_dimension=0,
        tiled=True,
    )
    projected = projected.astype(jnp.bfloat16).reshape(row_count, 3, head_width)
    local_heads = head_width // HEAD
    length = key_cache.shape[1] + 1
    source = jnp.arange(row_count, dtype=jnp.int32) // BEAMS * BEAMS + parents
    key_rows = jnp.concatenate(
        [jnp.take(key_cache, source, axis=0), projected[:, 1][:, None]], axis=1
    )
    value_rows = jnp.concatenate(
        [jnp.take(value_cache, source, axis=0), projected[:, 2][:, None]], axis=1
    )
    key_rows = key_rows.reshape(row_count, length, local_heads, HEAD)
    value_rows = value_rows.reshape(row_count, length, local_heads, HEAD)
    queries = projected[:, 0].reshape(row_count, local_heads, HEAD)
    scores = jnp.einsum(
        "thd,tjhd->thj", queries, key_rows, preferred_element_type=jnp.float32
    ) * HEAD ** (-0.5)
    softmax_w = jax.nn.softmax(scores, axis=-1).astype(jnp.bfloat16)
    attention_result = jnp.einsum(
        "thj,tjhd->thd", softmax_w, value_rows, preferred_element_type=jnp.float32
    )
    attention_result = attention_result.astype(jnp.bfloat16).reshape(row_count, head_width)
    partial_value = jnp.dot(
        attention_result,
        lax.all_gather(out_weight, "dp", axis=1, tiled=True),
        preferred_element_type=jnp.float32,
    )
    attn_out = lax.psum(partial_value, "mp")
    stream = tokens.astype(jnp.float32) + attn_out
    head_input = root_norm(stream, head_gain).astype(jnp.bfloat16)
    depth_rows = head_weight.shape[0]
    own_part = lax.dynamic_slice_in_dim(
        head_input, lax.axis_index("mp") * depth_rows, depth_rows, 1
    )
    partial_logits = jnp.dot(own_part, head_weight, preferred_element_type=jnp.float32)
    next_logits = lax.psum_scatter(
        select_blocks(partial_logits, allowed).astype(jnp.bfloat16),
        "mp",
        scatter_dimension=1,
        tiled=True,
    ).astype(jnp.float32)
    return (stream.astype(jnp.bfloat16), next_logits)


def solution(mesh):
    in_specs = (
        P("dp", None),
        P(),
        P(),
        P("dp", None, "mp"),
        P("mp", "dp"),
        P("mp", None),
        P("dp", None, "mp"),
        P("dp", None, "mp"),
        P("dp"),
        P("dp", None),
    )
    out_specs = (P("dp", None), P("dp", "mp"))
    return jax.shard_map(
        on_device, mesh=mesh, in_specs=in_specs, out_specs=out_specs, check_vma=False
    )
```

profile of v0, /device:TPU:0, one launch (start us, length us, event | category | flops | bytes accessed | tf_op | source)
XLA Modules:
  0.0 211.9 jit_solution(16103499963755374255)
XLA Ops:
  7.2 0.0 copy-start
  7.2 1.3 fusion.11
  8.5 1.1 fusion.13
  9.6 0.7 copy.55
  10.4 5.2 %all-to-all-start = ((bf16[40,8,512]{2,0,1:T(8,128)(2,1)}), bf16[40,8,512]{2,0,1:T(8,128)(2,1)S(1)}, u32[]{:S(2)}, u32[]{:S(2)}) async-start(bf16[40,8,512]{2,0,1:T(8,128)(2,1)} %bitcast.32), calls=%async_computation | async-start | bytes 655360 | tf_op jit(solution)/shard_map/all_to_all | solution.py:43
  15.6 0.0 reduce-scatter.5.cloned.1.call-start
  15.6 4.7 %copy.24 = bf16[512,3,1024]{0,2,1:T(8,128)(2,1)} copy(bf16[512,3,1024]{2,0,1:T(8,128)(2,1)} %param.15) | data formatting | bytes 6291456 | tf_op args[3]
  20.3 2.9 %all-to-all-done = bf16[40,8,512]{2,0,1:T(8,128)(2,1)S(1)} async-done(((bf16[40,8,512]{2,0,1:T(8,128)(2,1)}), bf16[40,8,512]{2,0,1:T(8,128)(2,1)S(1)}, u32[]{:S(2)}, u32[]{:S(2)}) %all-to-all-start) | async-done | bytes 327712 | tf_op jit(solution)/shard_map/all_to_all | solution.py:43
  23.2 0.0 copy-start.3
  23.2 5.0 %fusion.35 = f32[320,3072]{1,0:T(8,128)} fusion(bf16[320,512]{1,0:T(8,128)(2,1)S(1)} %bitcast.34, bf16[512,3072]{0,1:T(8,128)(2,1)} %bitcast.33), kind=kOutput, calls=%fused_computation.57 | convolution fusion | flops 1006632960 | bytes 7405568 | tf_op jit(solution)/shard_map/dot_general | solution.py:48
  28.2 0.0 reduce-scatter.5.cloned.1.call-update
  28.2 0.0 all-gather.2.cloned.1.call-start
  28.3 0.7 all-gather.2.cloned.1.call-update
  29.0 0.0 all-reduce.2.cloned.1.call-start
  29.0 0.0 copy-done.3
  29.1 7.2 %gather_fusion = bf16[40,64,1024]{2,1,0:T(8,128)(2,1)} fusion(bf16[40,64,1024]{2,1,0:T(8,128)(2,1)} %param.18, s32[1024]{0:T(1024)S(1)} %pad_clamp_fusion), kind=kCustom, calls=%fused_computation.clone | custom fusion | bytes 10485920 | tf_op jit(solution)/shard_map/jit(_take)/gather | solution.py:58
  36.3 7.6 %gather_fusion.1 = bf16[40,64,1024]{2,1,0:T(8,128)(2,1)} fusion(bf16[40,64,1024]{2,1,0:T(8,128)(2,1)} %param.19, s32[1024]{0:T(1024)S(1)} %pad_clamp_fusion), kind=kCustom, calls=%fused_computation.1.clone | custom fusion | bytes 10485920 | tf_op jit(solution)/shard_map/jit(_take)/gather | solution.py:61
  43.9 9.1 %broadcast_select_fusion.1 = (bf16[40,64,1024]{2,1,0:T(8,128)(2,1)}, bf16[40,64,1024]{2,1,0:T(8,128)(2,1)}) fusion(bf16[40,64,1024]{2,1,0:T(8,128)(2,1)} %gather_fusion, pred[40]{0:T(512)(128)(4,1)S(1)} %get-tuple-element.5, bf16[40,64,1024]{2,1,0:T(8,128)(2,1)} %gather_fusion.1), kind=kLoop, calls=%fused_computation.11 | loop fusion | flops 5242880 | bytes 20971560 | tf_op jit(solution)/shard_map/jit(_take)/select_n | solution.py:58
  52.9 24.6 %reduce-scatter.5.cloned.1.call-done = f32[40,3072]{1,0:T(8,128)} async-done(((f32[320,3072]{1,0:T(8,128)}), f32[40,3072]{1,0:T(8,128)}) %reduce-scatter.5.cloned.1.call-update) | async-done | bytes 491536 | tf_op jit(solution)/shard_map/reduce_scatter | solution.py:47
  77.6 1.1 convert_element_type.34
  78.6 0.4 reshape.54
  79.0 0.3 fusion.32
  79.3 11.1 %pad_maximum_fusion = (bf16[40,65,1024]{2,1,0:T(8,128)(2,1)}, bf16[40,65,1024]{2,1,0:T(8,128)(2,1)}) fusion(bf16[40,1,1024]{2,1,0:T(2,128)(2,1)S(1)} %get-tuple-element.7, bf16[40,64,1024]{2,1,0:T(8,128)(2,1)} %get-tuple-element.9, bf16[40,1,1024]{2,1,0:T(2,128)(2,1)S(1)} %get-tuple-element.8, bf16[40,64,1024]{2,1,0:T(8,128)(2,1)} %get-tuple-element.10), kind=kLoop, calls=%fused_computation.4 | loop fusion | flops 21299200 | bytes 21299200 | tf_op jit(solution)/shard_map/concatenate | solution.py:57
  90.4 9.1 %reshape.86 = bf16[40,65,8,128]{3,2,1,0:T(8,128)(2,1)} reshape(bf16[40,65,1024]{2,1,0:T(8,128)(2,1)} %get-tuple-element.11) | data formatting | bytes 10649600 | tf_op jit(solution)/shard_map/reshape | solution.py:63
  99.5 9.3 %reshape.87 = bf16[40,65,8,128]{3,2,1,0:T(8,128)(2,1)} reshape(bf16[40,65,1024]{2,1,0:T(8,128)(2,1)} %get-tuple-element.12) | data formatting | bytes 10649600 | tf_op jit(solution)/shard_map/reshape | solution.py:64
  108.8 5.9 %fusion.4 = f32[40,8,1,65]{3,2,1,0:T(1,128)S(1)} fusion(bf16[40,65,8,128]{3,2,1,0:T(8,128)(2,1)} %reshape.86, bf16[40,3,1024]{2,1,0:T(4,128)(2,1)S(1)} %reshape.54), kind=kOutput, calls=%fused_computation.8 | convolution fusion | flops 5324800 | bytes 5571840 | tf_op jit(solution)/shard_map/thd,tjhd->thj/dot_general | solution.py:66
  114.6 0.2 fusion.10
  114.9 4.2 %fusion.2 = f32[40,8,1,128]{3,2,1,0:T(1,128)S(1)} fusion(bf16[40,65,8,128]{3,2,1,0:T(8,128)(2,1)} %reshape.87, bf16[40,8,65,1]{2,1,0,3:T(8,128)(2,1)S(1)} %fusion.10), kind=kOutput, calls=%fused_computation.6 | convolution fusion | flops 5324800 | bytes 5530240 | tf_op jit(solution)/shard_map/thj,tjhd->thd/dot_general | solution.py:70
  119.1 16.2 %all-gather.2.cloned.1.call-done = bf16[1024,4096]{1,0:T(8,128)(2,1)} async-done(((bf16[1024,512]{1,0:T(8,128)(2,1)}), bf16[1024,4096]{1,0:T(8,128)(2,1)}) %all-gather.2.cloned.1.call-update) | async-done | bytes 8388624 | tf_op jit(solution)/shard_map/all_gather | solution.py:76
  135.3 0.0 copy-start.2
  135.3 5.9 %fusion.19 = f32[40,4096]{1,0:T(8,128)} fusion(bf16[1024,4096]{1,0:T(8,128)(2,1)} %all-gather.2.cloned.1.call-done, bf16[5,8,8,128]{3,2,1,0:T(8,128)(2,1)S(1)} %bitcast.36), kind=kOutput, calls=%fused_computation.34 | convolution fusion | flops 335544320 | bytes 9125888 | tf_op jit(solution)/shard_map/dot_general | solution.py:74
  141.2 0.0 all-reduce.2.cloned.1.call-update
  141.2 0.0 reduce-scatter.7.cloned.1.call-start
  141.3 0.0 copy-done.2
  141.3 0.1 copy.27
  141.4 0.7 dynamic-slice
  142.1 39.9 %all-reduce.2.cloned.1.call-done = f32[40,4096]{1,0:T(8,128)} async-done(((f32[40,4096]{1,0:T(8,128)}), f32[40,4096]{1,0:T(8,128)}) %all-reduce.2.cloned.1.call-update) | async-done | bytes 655376 | tf_op jit(solution)/shard_map/psum | solution.py:79
  181.9 0.0 copy-done.1
  181.9 1.3 multiply_reduce_fusion
  183.2 0.0 copy-done
  183.2 0.5 convolution_bitcast_fusion
  183.8 0.3 convolution_convert_fusion
  184.1 0.7 copy.40
  184.9 0.0 reduce-scatter.7.cloned.1.call-update
  184.9 0.8 convert_element_type.37
  185.7 18.2 %reduce-scatter.7.cloned.1.call-done = bf16[64,40]{1,0:T(8,128)(2,1)} async-done(((bf16[256,40]{1,0:T(8,128)(2,1)}), bf16[64,40]{1,0:T(8,128)(2,1)}) %reduce-scatter.7.cloned.1.call-update) | async-done | bytes 5136
  203.9 0.8 copy.39
  204.7 0.6 convert_element_type.41
  (7 shorter events, 0.1 us)
Async XLA Ops:
  7.2 176.1 %copy-start = (bf16[1024,1024]{1,0:T(8,128)(2,1)S(1)}, bf16[1024,1024]{1,0:T(8,128)(2,1)}, u32[]{:S(2)}) copy-start(bf16[1024,1024]{1,0:T(8,128)(2,1)} %param.17) | copy-start | bytes 6291460
  10.4 12.8 %all-to-all-start = ((bf16[40,8,512]{2,0,1:T(8,128)(2,1)}), bf16[40,8,512]{2,0,1:T(8,128)(2,1)S(1)}, u32[]{:S(2)}, u32[]{:S(2)}) async-start(bf16[40,8,512]{2,0,1:T(8,128)(2,1)} %bitcast.32), calls=%async_computation | async-start | bytes 655360 | tf_op jit(solution)/shard_map/all_to_all | solution.py:43
  15.6 62.0 %reduce-scatter.5.cloned.1.call-start = ((), (), s32[]{:S(2)}) async-start(), calls=%async_computation.3 | async-start | bytes 4423680 | tf_op jit(solution)/shard_map/reduce_scatter | solution.py:47
  23.2 5.8 %copy-start.3 = (s32[40]{0:T(128)S(1)}, s32[40]{0:T(128)}, u32[]{:S(2)}) copy-start(s32[40]{0:T(128)} %param.20) | copy-start | bytes 484
  28.2 107.1 %all-gather.2.cloned.1.call-start = ((), (), s32[]{:S(2)}) async-start(), calls=%async_computation.4 | async-start | bytes 9437184 | tf_op jit(solution)/shard_map/all_gather | solution.py:76
  29.0 153.0 %all-reduce.2.cloned.1.call-start = ((), (), s32[]{:S(2)}) async-start(), calls=%async_computation.5 | async-start | bytes 1310720 | tf_op jit(solution)/shard_map/psum | solution.py:79
  135.3 6.0 %copy-start.2 = (s32[40,2]{0,1:T(2,128)S(1)}, s32[40,2]{0,1:T(2,128)}, u32[]{:S(2)}) copy-start(s32[40,2]{0,1:T(2,128)} %param.21) | copy-start | bytes 964
  135.3 46.6 %copy-start.1 = (bf16[40,4096]{1,0:T(8,128)(2,1)S(1)}, bf16[40,4096]{1,0:T(8,128)(2,1)}, u32[]{:S(2)}) copy-start(bf16[40,4096]{1,0:T(8,128)(2,1)} %param.12) | copy-start | bytes 983044
  141.2 62.7 %reduce-scatter.7.cloned.1.call-start = ((), (), s32[]{:S(2)}) async-start(), calls=%async_computation.6 | async-start | bytes 81920
Sparse Core Ops, SparseCore 0:
  28.3 49.1 reduce-scatter.4
  79.4 55.8 all-gather.1
  141.4 40.5 all-reduce.1
  185.0 18.8 reduce-scatter.6
where the time goes:
time: 213 us; the launch traced here: 212 us
  waiting for transfers between devices  103 us (48%)
  local copies, waits for them, and re-layouts  41.6 us (20%)
  other arithmetic  26.6 us (12%)
  matrix products  21.8 us (10%)
  between operations  13.9 us (7%)
  starting transfers between devices  5.36 us (3%)
    psum x1, waiting for transfers between devices, on_device(): attn_out = lax.psum(partial_value, 'mp')  39.9 us
    reduce_scatter x1, waiting for transfers between devices, on_device(): lax.psum_scatter(jnp.dot(spread, flat_qkv, preferred_element_type=jnp.flo...  24.6 us
    unnamed x5, waiting for transfers between devices  19 us
    all_gather x1, waiting for transfers between devices, on_device(): lax.all_gather(out_weight, 'dp', axis=1, tiled=True)  16.2 us
    concatenate x1, other arithmetic, on_device(): jnp.concatenate([jnp.take(key_cache, source, axis=0), projected[:, 1][:,...  11.1 us
    reshape x1, local copies, waits for them, and re-layouts, on_device(): value_rows = value_rows.reshape(row_count, length, local_heads, HEAD)  9.25 us
    reshape x1, local copies, waits for them, and re-layouts, on_device(): key_rows = key_rows.reshape(row_count, length, local_heads, HEAD)  9.11 us
    select_n x1, other arithmetic, on_device(): jnp.take(key_cache, source, axis=0)  9.08 us
  transfers between devices with their start and end apart: 5, of which 5 were waited for; matrix products, arithmetic and copies ran while one was open for 34% of the time, Pallas kernels for 0%

commit v1 on v0

--- a/solution.py
+++ b/solution.py
@@ -6,6 +6,15 @@
 HEAD = 128
 BEAMS = 20
 BLOCK = 128
+
+
+def add_in_pairs(block, axis):
+    size = lax.axis_size(axis)
+    total, stride = (block, 1)
+    while stride < size:
+        total = total + lax.ppermute(total, axis, [(i, i ^ stride) for i in range(size)])
+        stride = 2 * stride
+    return total
 
 
 def root_norm(values, gain_vec):
@@ -76,7 +85,7 @@
         lax.all_gather(out_weight, "dp", axis=1, tiled=True),
         preferred_element_type=jnp.float32,
     )
-    attn_out = lax.psum(partial_value, "mp")
+    attn_out = add_in_pairs(partial_value, "mp")
     stream = tokens.astype(jnp.float32) + attn_out
     head_input = root_norm(stream, head_gain).astype(jnp.bfloat16)
     depth_rows = head_weight.shape[0]

time: 213 us -> 220 us (1.033)
  starting transfers between devices: 5.36 us -> 9.32 us
  waiting for transfers between devices: 103 us -> 106 us
    ppermute x0 -> x2, waiting for transfers between devices: none -> 43.3 us  [add_in_pairs(): lax.ppermute(total, axis, [(i, i ^ stride) for i in range(size)])]
    psum x1 -> x0, waiting for transfers between devices: 39.9 us -> none  [on_device(): attn_out = lax.psum(partial_value, 'mp')]
    ppermute x0 -> x2, starting transfers between devices: none -> 4.01 us  [add_in_pairs(): lax.ppermute(total, axis, [(i, i ^ stride) for i in range(size)])]
    unnamed x5 -> x4, waiting for transfers between devices: 19 us -> 19.4 us
    unnamed x13 -> x15, local copies, waits for them, and re-layouts: 6.34 us -> 6.34 us
  transfers between devices with their start and end apart: 5 -> 6, of which waited for: 5 -> 6; matrix products, arithmetic and copies ran while one was open for 34% -> 33% of each run, Pallas kernels for 0% -> 0%
where the time goes in v1:
time: 220 us; the launch traced here: 219 us
  waiting for transfers between devices  106 us (48%)
  local copies, waits for them, and re-layouts  41.6 us (19%)
  other arithmetic  26.9 us (12%)
  matrix products  20.9 us (10%)
  between operations  13.9 us (6%)
  starting transfers between devices  9.32 us (4%)
    ppermute x2, waiting for transfers between devices, add_in_pairs(): lax.ppermute(total, axis, [(i, i ^ stride) for i in range(size)])  43.3 us
    reduce_scatter x1, waiting for transfers between devices, on_device(): lax.psum_scatter(jnp.dot(spread, flat_qkv, preferred_element_type=jnp.flo...  24.6 us
    unnamed x4, waiting for transfers between devices  19.4 us
    all_gather x1, waiting for transfers between devices, on_device(): lax.all_gather(out_weight, 'dp', axis=1, tiled=True)  16.2 us
    concatenate x1, other arithmetic, on_device(): jnp.concatenate([jnp.take(key_cache, source, axis=0), projected[:, 1][:,...  11.1 us
    reshape x1, local copies, waits for them, and re-layouts, on_device(): value_rows = value_rows.reshape(row_count, length, local_heads, HEAD)  9.25 us
    reshape x1, local copies, waits for them, and re-layouts, on_device(): key_rows = key_rows.reshape(row_count, length, local_heads, HEAD)  9.12 us
    select_n x1, other arithmetic, on_device(): jnp.take(key_cache, source, axis=0)  9.08 us
  transfers between devices with their start and end apart: 6, of which 6 were waited for; matrix products, arithmetic and copies ran while one was open for 33% of the time, Pallas kernels for 0%

profile of v1, /device:TPU:0, one launch (start us, length us, event | category | flops | bytes accessed | tf_op | source)
XLA Modules:
  0.0 219.0 jit_solution(15246667602047859498)
XLA Ops:
  7.2 0.0 copy-start
  7.2 1.3 fusion.11
  8.5 1.1 fusion.13
  9.6 0.7 copy.55
  10.4 5.2 %all-to-all-start = ((bf16[40,8,512]{2,0,1:T(8,128)(2,1)}), bf16[40,8,512]{2,0,1:T(8,128)(2,1)S(1)}, u32[]{:S(2)}, u32[]{:S(2)}) async-start(bf16[40,8,512]{2,0,1:T(8,128)(2,1)} %bitcast.32), calls=%async_computation | async-start | bytes 655360 | tf_op jit(solution)/shard_map/all_to_all | solution.py:52
  15.6 0.0 reduce-scatter.5.cloned.1.call-start
  15.6 4.7 %copy.24 = bf16[512,3,1024]{0,2,1:T(8,128)(2,1)} copy(bf16[512,3,1024]{2,0,1:T(8,128)(2,1)} %param.15) | data formatting | bytes 6291456 | tf_op args[3]
  20.3 2.9 %all-to-all-done = bf16[40,8,512]{2,0,1:T(8,128)(2,1)S(1)} async-done(((bf16[40,8,512]{2,0,1:T(8,128)(2,1)}), bf16[40,8,512]{2,0,1:T(8,128)(2,1)S(1)}, u32[]{:S(2)}, u32[]{:S(2)}) %all-to-all-start) | async-done | bytes 327712 | tf_op jit(solution)/shard_map/all_to_all | solution.py:52
  23.2 5.0 %fusion.35 = f32[320,3072]{1,0:T(8,128)} fusion(bf16[320,512]{1,0:T(8,128)(2,1)S(1)} %bitcast.34, bf16[512,3072]{0,1:T(8,128)(2,1)} %bitcast.33), kind=kOutput, calls=%fused_computation.57 | convolution fusion | flops 1006632960 | bytes 7405568 | tf_op jit(solution)/shard_map/dot_general | solution.py:57
  28.2 0.0 reduce-scatter.5.cloned.1.call-update
  28.2 0.0 all-gather.2.cloned.1.call-start
  28.2 0.7 all-gather.2.cloned.1.call-update
  29.0 0.0 reduce-scatter.7.cloned.1.call-start
  29.0 0.0 copy-done.4
  29.0 7.2 %gather_fusion = bf16[40,64,1024]{2,1,0:T(8,128)(2,1)} fusion(bf16[40,64,1024]{2,1,0:T(8,128)(2,1)} %param.18, s32[1024]{0:T(1024)S(1)} %pad_clamp_fusion), kind=kCustom, calls=%fused_computation.clone | custom fusion | bytes 10485920 | tf_op jit(solution)/shard_map/jit(_take)/gather | solution.py:67
  36.3 7.6 %gather_fusion.1 = bf16[40,64,1024]{2,1,0:T(8,128)(2,1)} fusion(bf16[40,64,1024]{2,1,0:T(8,128)(2,1)} %param.19, s32[1024]{0:T(1024)S(1)} %pad_clamp_fusion), kind=kCustom, calls=%fused_computation.1.clone | custom fusion | bytes 10485920 | tf_op jit(solution)/shard_map/jit(_take)/gather | solution.py:70
  43.9 9.1 %broadcast_select_fusion.1 = (bf16[40,64,1024]{2,1,0:T(8,128)(2,1)}, bf16[40,64,1024]{2,1,0:T(8,128)(2,1)}) fusion(bf16[40,64,1024]{2,1,0:T(8,128)(2,1)} %gather_fusion, pred[40]{0:T(512)(128)(4,1)S(1)} %get-tuple-element.5, bf16[40,64,1024]{2,1,0:T(8,128)(2,1)} %gather_fusion.1), kind=kLoop, calls=%fused_computation.11 | loop fusion | flops 5242880 | bytes 20971560 | tf_op jit(solution)/shard_map/jit(_take)/select_n | solution.py:67
  52.9 24.6 %reduce-scatter.5.cloned.1.call-done = f32[40,3072]{1,0:T(8,128)} async-done(((f32[320,3072]{1,0:T(8,128)}), f32[40,3072]{1,0:T(8,128)}) %reduce-scatter.5.cloned.1.call-update) | async-done | bytes 491536 | tf_op jit(solution)/shard_map/reduce_scatter | solution.py:56
  77.6 1.1 convert_element_type.34
  78.6 0.4 reshape.54
  79.0 0.3 fusion.32
  79.3 11.1 %pad_maximum_fusion = (bf16[40,65,1024]{2,1,0:T(8,128)(2,1)}, bf16[40,65,1024]{2,1,0:T(8,128)(2,1)}) fusion(bf16[40,1,1024]{2,1,0:T(2,128)(2,1)S(1)} %get-tuple-element.7, bf16[40,64,1024]{2,1,0:T(8,128)(2,1)} %get-tuple-element.9, bf16[40,1,1024]{2,1,0:T(2,128)(2,1)S(1)} %get-tuple-element.8, bf16[40,64,1024]{2,1,0:T(8,128)(2,1)} %get-tuple-element.10), kind=kLoop, calls=%fused_computation.4 | loop fusion | flops 21299200 | bytes 21299200 | tf_op jit(solution)/shard_map/concatenate | solution.py:66
  90.4 9.1 %reshape.86 = bf16[40,65,8,128]{3,2,1,0:T(8,128)(2,1)} reshape(bf16[40,65,1024]{2,1,0:T(8,128)(2,1)} %get-tuple-element.11) | data formatting | bytes 10649600 | tf_op jit(solution)/shard_map/reshape | solution.py:72
  99.5 9.3 %reshape.87 = bf16[40,65,8,128]{3,2,1,0:T(8,128)(2,1)} reshape(bf16[40,65,1024]{2,1,0:T(8,128)(2,1)} %get-tuple-element.12) | data formatting | bytes 10649600 | tf_op jit(solution)/shard_map/reshape | solution.py:73
  108.8 5.9 %fusion.4 = f32[40,8,1,65]{3,2,1,0:T(1,128)S(1)} fusion(bf16[40,65,8,128]{3,2,1,0:T(8,128)(2,1)} %reshape.86, bf16[40,3,1024]{2,1,0:T(4,128)(2,1)S(1)} %reshape.54), kind=kOutput, calls=%fused_computation.8 | convolution fusion | flops 5324800 | bytes 5571840 | tf_op jit(solution)/shard_map/thd,tjhd->thj/dot_general | solution.py:75
  114.6 0.2 fusion.10
  114.9 4.2 %fusion.2 = f32[40,8,1,128]{3,2,1,0:T(1,128)S(1)} fusion(bf16[40,65,8,128]{3,2,1,0:T(8,128)(2,1)} %reshape.87, bf16[40,8,65,1]{2,1,0,3:T(8,128)(2,1)S(1)} %fusion.10), kind=kOutput, calls=%fused_computation.6 | convolution fusion | flops 5324800 | bytes 5530240 | tf_op jit(solution)/shard_map/thj,tjhd->thd/dot_general | solution.py:79
  119.1 16.2 %all-gather.2.cloned.1.call-done = bf16[1024,4096]{1,0:T(8,128)(2,1)} async-done(((bf16[1024,512]{1,0:T(8,128)(2,1)}), bf16[1024,4096]{1,0:T(8,128)(2,1)}) %all-gather.2.cloned.1.call-update) | async-done | bytes 8388624 | tf_op jit(solution)/shard_map/all_gather | solution.py:85
  135.3 5.0 %fusion.19 = f32[40,4096]{1,0:T(8,128)S(1)} fusion(bf16[1024,4096]{1,0:T(8,128)(2,1)} %all-gather.2.cloned.1.call-done, bf16[5,8,8,128]{3,2,1,0:T(8,128)(2,1)S(1)} %bitcast.36), kind=kOutput, calls=%fused_computation.34 | convolution fusion | flops 335544320 | bytes 9125888 | tf_op jit(solution)/shard_map/dot_general | solution.py:83
  140.3 1.5 collective-permute-start
  141.8 15.4 %collective-permute-done = f32[40,4096]{1,0:T(8,128)S(1)} collective-permute-done((f32[40,4096]{1,0:T(8,128)S(1)}, f32[40,4096]{1,0:T(8,128)S(1)}, u32[]{:S(2)}, u32[]{:S(2)}) %collective-permute-start) | collective-permute-done | bytes 655392 | tf_op jit(solution)/shard_map/ppermute | solution.py:15
  157.2 0.1 add.44
  157.3 0.0 copy-start.2
  157.3 2.5 %collective-permute-start.1 = (f32[40,4096]{1,0:T(8,128)S(1)}, f32[40,4096]{1,0:T(8,128)}, u32[]{:S(2)}, u32[]{:S(2)}) collective-permute-start(f32[40,4096]{1,0:T(8,128)S(1)} %add.44), channel_id=1, source_target_pairs={{0,2},{1,3},{2,0},{3,1},{4,6},{5,7},{6,4},{7,5},{8,10},{9,11},{10,... | collective-permute-start | bytes 1966088 | tf_op jit(solution)/shard_map/ppermute | solution.py:15
  159.8 0.0 copy-done.3
  159.8 0.1 copy.27
  159.9 0.7 dynamic-slice
  160.6 0.0 copy-done.2
  160.6 27.9 %collective-permute-done.1 = f32[40,4096]{1,0:T(8,128)} collective-permute-done((f32[40,4096]{1,0:T(8,128)S(1)}, f32[40,4096]{1,0:T(8,128)}, u32[]{:S(2)}, u32[]{:S(2)}) %collective-permute-start.1) | collective-permute-done | bytes 655392 | tf_op jit(solution)/shard_map/ppermute | solution.py:15
  188.5 1.5 multiply_reduce_fusion
  190.0 0.5 convolution_bitcast_fusion
  190.5 0.3 convolution_convert_fusion
  190.9 0.7 copy.40
  191.6 0.0 reduce-scatter.7.cloned.1.call-update
  191.7 0.8 convert_element_type.37
  192.4 18.7 %reduce-scatter.7.cloned.1.call-done = bf16[64,40]{1,0:T(8,128)(2,1)} async-done(((bf16[256,40]{1,0:T(8,128)(2,1)}), bf16[64,40]{1,0:T(8,128)(2,1)}) %reduce-scatter.7.cloned.1.call-update) | async-done | bytes 5136
  211.1 0.8 copy.39
  211.9 0.6 convert_element_type.41
  (11 shorter events, 0.1 us)
Async XLA Ops:
  7.2 182.8 %copy-start = (bf16[1024,1024]{1,0:T(8,128)(2,1)S(1)}, bf16[1024,1024]{1,0:T(8,128)(2,1)}, u32[]{:S(2)}) copy-start(bf16[1024,1024]{1,0:T(8,128)(2,1)} %param.17) | copy-start | bytes 6291460
  10.4 12.8 %all-to-all-start = ((bf16[40,8,512]{2,0,1:T(8,128)(2,1)}), bf16[40,8,512]{2,0,1:T(8,128)(2,1)S(1)}, u32[]{:S(2)}, u32[]{:S(2)}) async-start(bf16[40,8,512]{2,0,1:T(8,128)(2,1)} %bitcast.32), calls=%async_computation | async-start | bytes 655360 | tf_op jit(solution)/shard_map/all_to_all | solution.py:52
  15.6 62.0 %reduce-scatter.5.cloned.1.call-start = ((), (), s32[]{:S(2)}) async-start(), calls=%async_computation.3 | async-start | bytes 4423680 | tf_op jit(solution)/shard_map/reduce_scatter | solution.py:56
  23.2 5.8 %copy-start.4 = (s32[40]{0:T(128)S(1)}, s32[40]{0:T(128)}, u32[]{:S(2)}) copy-start(s32[40]{0:T(128)} %param.20) | copy-start | bytes 484
  28.2 107.1 %all-gather.2.cloned.1.call-start = ((), (), s32[]{:S(2)}) async-start(), calls=%async_computation.4 | async-start | bytes 9437184 | tf_op jit(solution)/shard_map/all_gather | solution.py:85
  29.0 182.1 %reduce-scatter.7.cloned.1.call-start = ((), (), s32[]{:S(2)}) async-start(), calls=%async_computation.5 | async-start | bytes 81920
  135.3 24.5 %copy-start.3 = (s32[40,2]{0,1:T(2,128)S(1)}, s32[40,2]{0,1:T(2,128)}, u32[]{:S(2)}) copy-start(s32[40,2]{0,1:T(2,128)} %param.21) | copy-start | bytes 964
  135.3 53.1 %copy-start.1 = (bf16[40,4096]{1,0:T(8,128)(2,1)S(1)}, bf16[40,4096]{1,0:T(8,128)(2,1)}, u32[]{:S(2)}) copy-start(bf16[40,4096]{1,0:T(8,128)(2,1)} %param.12) | copy-start | bytes 983044
  140.3 16.9 %collective-permute-start = (f32[40,4096]{1,0:T(8,128)S(1)}, f32[40,4096]{1,0:T(8,128)S(1)}, u32[]{:S(2)}, u32[]{:S(2)}) collective-permute-start(f32[40,4096]{1,0:T(8,128)S(1)} %fusion.19), channel_id=1, source_target_pairs={{0,1},{1,0},{2,3},{3,2},{4,5},{5,4},{6,7},{7,6},{8,9},{9,8},{10,11... | collective-permute-start | bytes 1966088 | tf_op jit(solution)/shard_map/ppermute | solution.py:15
  157.3 3.3 %copy-start.2 = (f32[40,4096]{1,0:T(8,128)}, f32[40,4096]{1,0:T(8,128)S(1)}, u32[]{:S(2)}) copy-start(f32[40,4096]{1,0:T(8,128)S(1)} %add.44) | copy-start | bytes 1966084
  157.3 31.1 %collective-permute-start.1 = (f32[40,4096]{1,0:T(8,128)S(1)}, f32[40,4096]{1,0:T(8,128)}, u32[]{:S(2)}, u32[]{:S(2)}) collective-permute-start(f32[40,4096]{1,0:T(8,128)S(1)} %add.44), channel_id=1, source_target_pairs={{0,2},{1,3},{2,0},{3,1},{4,6},{5,7},{6,4},{7,5},{8,10},{9,11},{10,... | collective-permute-start | bytes 1966088 | tf_op jit(solution)/shard_map/ppermute | solution.py:15
Sparse Core Ops, SparseCore 0:
  28.3 49.1 reduce-scatter.4
  79.4 55.8 all-gather.1
  191.8 19.2 reduce-scatter.6
